TPU v7x, 512 devices: a whole 4x4x16 slice. The times are simulated.
512 devices in a mesh: dp: 64 (over x, z), tensor: 8 (over y, core).
Axes of the slice: x: 4, y: 4, z: 16, core: 2. Of those that a mesh axis runs over, the one named last changes fastest.
Arguments:
- tokens: bfloat16 [8192, 8192], P('dp', 'tensor'), may hold values from -6 to 6
- hidden_grad: bfloat16 [8192, 28672], P('dp', 'tensor'), may hold values from -0.0625 to 0.0625
- masters: float32 [8, 64, 128, 128], P('tensor', 'dp'), may hold values from -0.5 to 0.5
- block_row: int32 [8, 32], P('tensor'), may hold values from 0 to 63, as said below
- block_col: int32 [8, 32], P('tensor'), may hold values from 0 to 27
- owners: int32 [8, 64], P('tensor'), may hold values from 0 to 63, as said below
Outputs:
- grads: float32 [8, 192, 128, 128], P('tensor', 'dp')
Inputs may be any that keep to these rules, and one draw needn't show every extreme that they name: `block_row`: in each slice the kept places are distinct. `owners`: in each slice every owner takes at most 3 of the 64 kept blocks, and some owner takes exactly 3.
All inputs are finite; a program needn't handle non-finite values.
Results may differ from a plain program's by a relative error of at most 0.0044.
Values may be sent and summed in bfloat16 or wider, within the bound.
A program may use at most 64 MiB of HBM per device.

v0:
```python
import jax
import jax.numpy as jnp
from jax import lax
from jax.sharding import PartitionSpec as P


def slot_index(owner_row, capacity):
    count_all = owner_row.shape[0]
    same_owner = owner_row[:, None] == owner_row[None, :]
    earlier = (
        jnp.arange(count_all, dtype=jnp.int32)[None, :]
        < jnp.arange(count_all, dtype=jnp.int32)[:, None]
    )
    rank_index = jnp.sum(
        jnp.logical_and(same_owner, earlier).astype(jnp.int32), axis=1, dtype=jnp.int32
    )
    return owner_row * capacity + rank_index


def column_total(part, same_column):
    return jnp.einsum("tjc,kj->tkc", part, same_column, precision=lax.Precision.HIGHEST)


def local(tokens, hidden_grad, masters, block_row, block_col, owners):
    high = lax.Precision.HIGHEST
    features = lax.all_gather(tokens, "tensor", axis=1, tiled=True)
    token_count = features.shape[0]
    block_side = masters.shape[-1]
    kept_count = block_row.shape[1]
    weights = lax.all_gather(masters.astype(jnp.bfloat16), "dp", axis=1, tiled=True)[0]
    row_index = block_row[0]
    column_index = block_col[0]
    by_block = features.reshape(token_count, features.shape[1] // block_side, block_side)
    selected = jnp.take(by_block, row_index, axis=1)
    gate_part = jnp.einsum(
        "tkb,kbc->tkc", selected, weights[:kept_count], preferred_element_type=jnp.float32
    )
    up_part = jnp.einsum(
        "tkb,kbc->tkc", selected, weights[kept_count:], preferred_element_type=jnp.float32
    )
    same_column = (column_index[:, None] == column_index[None, :]).astype(jnp.float32)
    gate_value = column_total(gate_part, same_column)
    up_value = column_total(up_part, same_column)
    grad_columns = hidden_grad.reshape(token_count, hidden_grad.shape[1] // block_side, block_side)
    upstream = jnp.take(grad_columns, column_index, axis=1).astype(jnp.float32)
    sigmoid_gate = jax.nn.sigmoid(gate_value)
    gate_grad = (
        upstream * up_value * sigmoid_gate * (1.0 + gate_value * (1.0 - sigmoid_gate))
    ).astype(jnp.bfloat16)
    up_grad = (upstream * gate_value * sigmoid_gate).astype(jnp.bfloat16)
    grad_gate = jnp.einsum("tkb,tkc->kbc", selected, gate_grad, preferred_element_type=jnp.float32)
    grad_up = jnp.einsum("tkb,tkc->kbc", selected, up_grad, preferred_element_type=jnp.float32)
    block_grads = jnp.concatenate([grad_gate, grad_up], axis=0)
    owner_count = lax.axis_size("dp")
    capacity = 3 * block_grads.shape[0] // owner_count
    slot_list = slot_index(owners[0], capacity)
    summed = lax.psum(block_grads, "dp")
    own_slots = lax.axis_index("dp") * capacity + jnp.arange(capacity, dtype=jnp.int32)
    selector = (own_slots[:, None] == slot_list[None, :]).astype(jnp.float32)
    result = jnp.einsum("sk,kbc->sbc", selector, summed, precision=high)
    return result[None]


def solution(mesh):
    return jax.shard_map(
        local,
        mesh=mesh,
        in_specs=(
            P("dp", "tensor"),
            P("dp", "tensor"),
            P("tensor", "dp", None, None),
            P("tensor", None),
            P("tensor", None),
            P("tensor", None),
        ),
        out_specs=P("tensor", "dp", None, None),
        check_vma=False,
    )
```

profile of v0, /device:TPU:8, one launch (start us, length us, event | category | flops | bytes accessed | tf_op | source)
XLA Modules:
  0.0 505.0 jit_solution(9367897133489525281)
XLA Ops:
  6.5 0.0 all-gather.3.cloned.1.call-start
  6.5 1.8 copy.48
  8.3 0.0 all-gather.3.cloned.1.call-update
  8.4 0.0 all-gather.5.cloned.1.call-start
  8.4 1.5 bitcast_convert_fusion
  9.9 0.0 all-gather.5.cloned.1.call-update
  9.9 0.0 all-reduce.2.cloned.1.call-start
  10.0 1.6 copy.51
  11.5 0.0 copy-start.2
  11.5 0.6 copy.52
  12.2 1.6 gather_fusion.1
  13.9 31.9 %all-gather.3.cloned.1.call-done = bf16[128,8192]{0,1:T(8,128)(2,1)} async-done(((bf16[128,1024]{0,1:T(8,128)(2,1)}), bf16[128,8192]{0,1:T(8,128)(2,1)}) %all-gather.3.cloned.1.call-update) | async-done | bytes 2097168 | tf_op jit(solution)/shard_map/all_gather | solution.py:26
  45.8 3.2 copy.49
  49.1 0.7 gather_fusion
  49.8 0.6 fusion.24
  50.5 1.2 copy.61
  51.7 139.4 %all-gather.5.cloned.1.call-done = bf16[1,64,128,128]{3,2,0,1:T(8,128)(2,1)} async-done(((bf16[1,1,128,128]{3,2,0,1:T(8,128)(2,1)}), bf16[1,64,128,128]{3,2,0,1:T(8,128)(2,1)}) %all-gather.5.cloned.1.call-update) | async-done | bytes 2097168 | tf_op jit(solution)/shard_map/all_gather | solution.py:30
  191.0 1.9 convolution_bitcast_fusion
  192.9 0.0 copy-done
  193.0 0.5 convolution_bitcast_fusion.1
  193.5 0.7 copy-done.1
  194.2 3.5 fusion.9
  197.7 3.8 fusion.7
  201.5 0.8 fusion.22
  202.2 0.8 fusion.20
  203.0 2.5 pad_maximum_fusion
  205.5 0.0 all-reduce.2.cloned.1.call-update
  205.5 0.6 copy-done.4
  206.1 0.2 convert_reduce_fusion
  206.3 285.7 %all-reduce.2.cloned.1.call-done = f32[64,128,128]{2,1,0:T(8,128)} async-done(((f32[64,128,128]{2,1,0:T(8,128)}), f32[64,128,128]{2,1,0:T(8,128)}) %all-reduce.2.cloned.1.call-update) | async-done | bytes 4194320 | tf_op jit(solution)/shard_map/psum | solution.py:57
  492.0 5.8 %fusion.17 = f32[1,3,128,128]{3,1,2,0:T(4,128)S(1)} fusion(f32[64,128,128]{2,1,0:T(8,128)} %all-reduce.2.cloned.1.call-done, s32[64]{0:T(128)S(1)} %fusion.40, s32[3]{0:T(128)S(1)} %iota_add_fusion), kind=kOutput, calls=%fused_computation.24 | convolution fusion | flops 37748928 | bytes 4391180 | tf_op jit(solution)/shard_map/sk,kbc->sbc/dot_general | solution.py:60
  497.8 0.7 copy.66
  (14 shorter events, 0.1 us)
Async XLA Ops:
  6.5 39.3 %all-gather.3.cloned.1.call-start = ((), (), s32[]{:S(2)}) async-start(), calls=%async_computation | async-start | bytes 2359296 | tf_op jit(solution)/shard_map/all_gather | solution.py:26
  8.3 3.8 copy-start.3
  8.4 182.7 %all-gather.5.cloned.1.call-start = ((), (), s32[]{:S(2)}) async-start(), calls=%async_computation.1 | async-start | bytes 2129920 | tf_op jit(solution)/shard_map/all_gather | solution.py:30
  9.9 482.1 %all-reduce.2.cloned.1.call-start = ((), (), s32[]{:S(2)}) async-start(), calls=%async_computation.2 | async-start | bytes 8388608 | tf_op jit(solution)/shard_map/psum | solution.py:57
  11.5 2.3 copy-start.2
  191.0 1.9 copy-start
  192.9 1.2 copy-start.1
  205.5 0.7 copy-start.4
Sparse Core Ops, SparseCore 0:
  9.5 36.2 all-gather.2
  48.8 142.2 all-gather.4
  205.6 286.3 all-reduce.1
where the time goes:
time: 505 us
  waiting for transfers between devices  457 us (90%)
  matrix products  17 us (3%)
  between operations  13.3 us (3%)
  local copies, waits for them, and re-layouts  12.8 us (3%)
    psum x1, waiting for transfers between devices, local(): summed = lax.psum(block_grads, 'dp')  286 us
    all_gather x1, waiting for transfers between devices, local(): lax.all_gather(masters.astype(jnp.bfloat16), 'dp', axis=1, tiled=True)[0]  139 us
    all_gather x1, waiting for transfers between devices, local(): features = lax.all_gather(tokens, 'tensor', axis=1, tiled=True)  31.9 us
  transfers between devices with their start and end apart: 3, of which 3 were waited for; matrix products, arithmetic and copies ran while one was open for 2% of the time, Pallas kernels for 0%

commit v1 on v0

--- a/solution.py
+++ b/solution.py
@@ -2,6 +2,27 @@
 import jax.numpy as jnp
 from jax import lax
 from jax.sharding import PartitionSpec as P
+
+
+def gather_around(array, axis, dim):
+    devices, mine, width = (lax.axis_size(axis), lax.axis_index(axis), array.shape[dim])
+    upward = [(i, (i + 1) % devices) for i in range(devices)]
+    backward = [(i, (i - 1) % devices) for i in range(devices)]
+    result = jnp.zeros((*array.shape[:dim], devices * width, *array.shape[dim + 1 :]), array.dtype)
+    result = lax.dynamic_update_slice_in_dim(result, array, mine * width, axis=dim)
+    from_left = from_right = array
+    half = devices // 2
+    for step in range(1, half + 1):
+        from_left = lax.ppermute(from_left, axis, upward)
+        result = lax.dynamic_update_slice_in_dim(
+            result, from_left, (mine - step) % devices * width, axis=dim
+        )
+        if step < devices - half:
+            from_right = lax.ppermute(from_right, axis, backward)
+            result = lax.dynamic_update_slice_in_dim(
+                result, from_right, (mine + step) % devices * width, axis=dim
+            )
+    return result
 
 
 def slot_index(owner_row, capacity):
@@ -23,7 +44,7 @@
 
 def local(tokens, hidden_grad, masters, block_row, block_col, owners):
     high = lax.Precision.HIGHEST
-    features = lax.all_gather(tokens, "tensor", axis=1, tiled=True)
+    features = gather_around(tokens, "tensor", 1)
     token_count = features.shape[0]
     block_side = masters.shape[-1]
     kept_count = block_row.shape[1]

time: 505 us -> 470 us (0.931)
  waiting for transfers between devices: 457 us -> 405 us
  starting transfers between devices: 0.09 us -> 8.97 us
    all_gather x1 -> x0, waiting for transfers between devices: 31.9 us -> none  [local(): features = lax.all_gather(tokens, 'tensor', axis=1, tiled=True)]
    all_gather x1, waiting for transfers between devices: 139 us -> 111 us  [local(): lax.all_gather(masters.astype(jnp.bfloat16), 'dp', axis=1, tiled=True)[0]]
    ppermute x0 -> x7, starting transfers between devices: none -> 8.93 us  [the longest x3 8.9 us: gather_around(): from_right = lax.ppermute(from_right, axis, backward)]
    ppermute x0 -> x7, waiting for transfers between devices: none -> 7.91 us  [the longest x4 7.9 us: gather_around(): from_left = lax.ppermute(from_left, axis, upward)]
  transfers between devices with their start and end apart: 3 -> 9, of which waited for: 3 -> 5; matrix products, arithmetic and copies ran while one was open for 2% -> 4% of each run, Pallas kernels for 0% -> 0%
where the time goes in v1:
time: 470 us
  waiting for transfers between devices  405 us (86%)
  local copies, waits for them, and re-layouts  17.5 us (4%)
  matrix products  16.8 us (4%)
  between operations  13.7 us (3%)
  starting transfers between devices  8.97 us (2%)
  other arithmetic  8.02 us (2%)
    psum x1, waiting for transfers between devices, local(): summed = lax.psum(block_grads, 'dp')  286 us
    all_gather x1, waiting for transfers between devices, local(): lax.all_gather(masters.astype(jnp.bfloat16), 'dp', axis=1, tiled=True)[0]  111 us
  transfers between devices with their start and end apart: 9, of which 5 were waited for; matrix products, arithmetic and copies ran while one was open for 4% of the time, Pallas kernels for 0%

profile of v1, /device:TPU:8, one launch (start us, length us, event | category | flops | bytes accessed | tf_op | source)
XLA Modules:
  0.0 469.9 jit_solution(285779372876205175)
XLA Ops:
  6.5 1.5 bitcast_convert_fusion
  8.2 1.1 copy.52
  9.3 1.7 collective-permute-start.1
  11.0 0.7 fusion.38
  11.7 0.7 compare_and_fusion.1
  12.4 0.7 fusion.39
  13.0 1.2 compare_and_fusion
  14.2 1.0 collective-permute-done
  15.6 3.2 collective-permute-start.3
  18.8 1.3 copy.57
  20.1 1.6 copy.58
  21.7 1.7 gather_fusion.1
  23.4 1.0 constant_dynamic-update-slice_fusion.6
  24.4 3.9 collective-permute-start.5
  28.4 1.0 constant_dynamic-update-slice_fusion.4
  29.4 2.2 collective-permute-done.4
  31.6 1.0 constant_dynamic-update-slice_fusion.3
  32.7 4.7 collective-permute-done.6
  37.4 2.9 copy.55
  40.3 2.3 gather_fusion
  43.3 1.2 copy.67
  44.5 111.2 %all-gather.2.cloned.1.call-done = bf16[1,64,128,128]{3,2,0,1:T(8,128)(2,1)} async-done(((bf16[1,1,128,128]{3,2,0,1:T(8,128)(2,1)}), bf16[1,64,128,128]{3,2,0,1:T(8,128)(2,1)}) %all-gather.2.cloned.1.call-update) | async-done | bytes 2097168 | tf_op jit(solution)/shard_map/all_gather | solution.py:51
  155.6 1.9 convolution_bitcast_fusion
  158.1 0.7 copy-done.1
  158.8 3.4 fusion.9
  162.2 3.7 fusion.7
  165.9 0.8 fusion.22
  166.7 0.8 fusion.20
  167.4 2.5 pad_maximum_fusion
  170.7 285.9 %all-reduce.2.cloned.1.call-done = f32[64,128,128]{2,1,0:T(8,128)} async-done(((f32[64,128,128]{2,1,0:T(8,128)}), f32[64,128,128]{2,1,0:T(8,128)}) %all-reduce.2.cloned.1.call-update) | async-done | bytes 4194320 | tf_op jit(solution)/shard_map/psum | solution.py:78
  456.6 5.8 %fusion.17 = f32[1,3,128,128]{3,1,2,0:T(4,128)S(1)} fusion(f32[64,128,128]{2,1,0:T(8,128)} %all-reduce.2.cloned.1.call-done, s32[64]{0:T(128)S(1)} %fusion.40, s32[3]{0:T(128)S(1)} %iota_add_fusion), kind=kOutput, calls=%fused_computation.24 | convolution fusion | flops 37748928 | bytes 4391180 | tf_op jit(solution)/shard_map/sk,kbc->sbc/dot_general | solution.py:81
  462.4 0.7 copy.72
  (36 shorter events, 2.6 us)
Async XLA Ops:
  6.5 12.3 %copy-start.2 = (bf16[128,3584]{1,0:T(8,128)(2,1)S(1)}, bf16[128,3584]{1,0:T(8,128)(2,1)}, u32[]{:S(2)}) copy-start(bf16[128,3584]{1,0:T(8,128)(2,1)} %param.7) | copy-start | bytes 2752516
  6.5 149.1 %all-gather.2.cloned.1.call-start = ((), (), s32[]{:S(2)}) async-start(), calls=%async_computation | async-start | bytes 2129920 | tf_op jit(solution)/shard_map/all_gather | solution.py:51
  8.1 448.5 %all-reduce.2.cloned.1.call-start = ((), (), s32[]{:S(2)}) async-start(), calls=%async_computation.1 | async-start | bytes 8388608 | tf_op jit(solution)/shard_map/psum | solution.py:78
  9.3 5.9 %collective-permute-start = (bf16[128,1024]{0,1:T(8,128)(2,1)S(1)}, bf16[128,1024]{0,1:T(8,128)(2,1)}, u32[]{:S(2)}, u32[]{:S(2)}) collective-permute-start(bf16[128,1024]{0,1:T(8,128)(2,1)S(1)} %copy.52), channel_id=1, source_target_pairs={{0,1},{1,2},{2,3},{3,4},{4,5},{5,6},{6,7},{7,0},{8,9},{9,10},{10,1... | collective-permute-start | bytes 786440 | tf_op jit(solution)/shard_map/ppermute | solution.py:16
  9.3 6.2 %collective-permute-start.1 = (bf16[128,1024]{0,1:T(8,128)(2,1)S(1)}, bf16[128,1024]{0,1:T(8,128)(2,1)S(1)}, u32[]{:S(2)}, u32[]{:S(2)}) collective-permute-start(bf16[128,1024]{0,1:T(8,128)(2,1)S(1)} %copy.52), channel_id=1, source_target_pairs={{0,7},{1,0},{2,1},{3,2},{4,3},{5,4},{6,5},{7,6},{8,15},{9,8},{10,9... | collective-permute-start | bytes 786440 | tf_op jit(solution)/shard_map/ppermute | solution.py:21
  15.2 8.2 %collective-permute-start.2 = (bf16[128,1024]{0,1:T(8,128)(2,1)}, bf16[128,1024]{0,1:T(8,128)(2,1)}, u32[]{:S(2)}, u32[]{:S(2)}) collective-permute-start(bf16[128,1024]{0,1:T(8,128)(2,1)} %collective-permute-done), channel_id=1, source_target_pairs={{0,1},{1,2},{2,3},{3,4},{4,5},{5,6},{6,7},{7,0},{8,9},{9,10},{10,1... | collective-permute-start | bytes 786440 | tf_op jit(solution)/shard_map/ppermute | solution.py:16
  15.6 8.9 %collective-permute-start.3 = (bf16[128,1024]{0,1:T(8,128)(2,1)S(1)}, bf16[128,1024]{0,1:T(8,128)(2,1)}, u32[]{:S(2)}, u32[]{:S(2)}) collective-permute-start(bf16[128,1024]{0,1:T(8,128)(2,1)S(1)} %collective-permute-done.1), channel_id=1, source_target_pairs={{0,7},{1,0},{2,1},{3,2},{4,3},{5,4},{6,5},{7,6},{8,15},{9,8},{10,9... | collective-permute-start | bytes 786440 | tf_op jit(solution)/shard_map/ppermute | solution.py:21
  23.4 8.2 %collective-permute-start.4 = (bf16[128,1024]{0,1:T(8,128)(2,1)}, bf16[128,1024]{0,1:T(8,128)(2,1)S(1)}, u32[]{:S(2)}, u32[]{:S(2)}) collective-permute-start(bf16[128,1024]{0,1:T(8,128)(2,1)} %collective-permute-done.2), channel_id=1, source_target_pairs={{0,1},{1,2},{2,3},{3,4},{4,5},{5,6},{6,7},{7,0},{8,9},{9,10},{10,1... | collective-permute-start | bytes 786440 | tf_op jit(solution)/shard_map/ppermute | solution.py:16
  24.4 8.2 %collective-permute-start.5 = (bf16[128,1024]{0,1:T(8,128)(2,1)}, bf16[128,1024]{0,1:T(8,128)(2,1)S(1)}, u32[]{:S(2)}, u32[]{:S(2)}) collective-permute-start(bf16[128,1024]{0,1:T(8,128)(2,1)} %collective-permute-done.3), channel_id=1, source_target_pairs={{0,7},{1,0},{2,1},{3,2},{4,3},{5,4},{6,5},{7,6},{8,15},{9,8},{10,9... | collective-permute-start | bytes 786440 | tf_op jit(solution)/shard_map/ppermute | solution.py:21
  31.6 5.8 %collective-permute-start.6 = (bf16[128,1024]{0,1:T(8,128)(2,1)S(1)}, bf16[128,1024]{0,1:T(8,128)(2,1)S(1)}, u32[]{:S(2)}, u32[]{:S(2)}) collective-permute-start(bf16[128,1024]{0,1:T(8,128)(2,1)S(1)} %collective-permute-done.4), channel_id=1, source_target_pairs={{0,1},{1,2},{2,3},{3,4},{4,5},{5,6},{6,7},{7,0},{8,9},{9,10},{10,1... | collective-permute-start | bytes 786440 | tf_op jit(solution)/shard_map/ppermute | solution.py:16
  155.6 1.9 copy-start
  157.5 1.2 copy-start.1
  157.6 1.2 copy-start.3
  157.6 1.2 copy-start.5
  169.9 0.7 copy-start.4
Sparse Core Ops, SparseCore 0:
  10.3 145.2 all-gather.1
  170.1 286.4 all-reduce.1
